TPU v7x, 32 devices: a whole 2x2x4 slice. The times are simulated.
32 devices in a mesh: ctx: 8 (over y, x, core), ch: 4 (over z).
Axes of the slice: x: 2, y: 2, z: 4, core: 2. Of those that a mesh axis runs over, the one named last changes fastest.
Arguments:
- q_short: bfloat16 [1024, 8192], P('ctx', 'ch'), may hold values from -6 to 6
- k_short: bfloat16 [1024, 8192], P('ctx', 'ch'), may hold values from -6 to 6
- v_input: bfloat16 [1024, 8192], P('ctx', 'ch'), may hold values from -6 to 6
- q_long: bfloat16 [1024, 8192], P('ctx', 'ch'), may hold values from -6 to 6
- k_long: bfloat16 [1024, 8192], P('ctx', 'ch'), may hold values from -6 to 6
- short_filter: bfloat16 [128, 512], P(None, 'ch'), may hold values from -0.5 to 0.5
- decay_rates: float32 [512, 16], P('ch'), may hold values from 0.0001953125 to 0.04
- residues: float32 [512, 16], P('ch'), may hold values from -1.5 to 1.5
Outputs:
- mixed: bfloat16 [1024, 8192], P('ctx', 'ch')
All inputs are finite; a program needn't handle non-finite values.
Results may differ from a plain program's by a relative error of at most 0.0065.
Values may be sent and summed in bfloat16 or wider, within the bound.
A program may use at most 64 MiB of HBM per device.

v0:
```python
import functools

import jax
import jax.numpy as jnp
from jax import lax
from jax.experimental import pallas as pl
from jax.experimental.pallas import tpu as pltpu
from jax.sharding import PartitionSpec as P

MESH = pl.DeviceIdType.MESH
LANES = 128
F32 = jnp.float32
BF16 = jnp.bfloat16


def iota(shape, dim):
    return lax.broadcasted_iota(jnp.int32, shape, dim)


def split(x):
    hi = x.astype(BF16)
    return hi, (x - hi.astype(F32)).astype(BF16)


def kernel(
    n, chunks, q_short, k_short, v_input, q_long, k_long, taps, rates, weights, out,
    ubuf, ulong, ynear, short_tab, long_tab, in_tab, out_tab, lam_rc, short_row, long_row, modes,
    state, psend, precv, halo_send, halo_recv, scan_send, scan_recv,
):
    me = lax.axis_index("ctx")
    tokens, ch = q_short.shape
    groups, order = rates.shape
    share = ch // groups
    per = LANES // share
    blocks = ch // LANES
    per_chunk = blocks // chunks
    width = per_chunk * LANES
    levels = n.bit_length() - 1

    barrier = pltpu.get_barrier_semaphore()
    for step in range(1, n):
        pl.semaphore_signal(
            barrier, inc=1, device_id={"ctx": lax.rem(me + step, n)}, device_id_type=MESH
        )

    ubuf[pl.ds(tokens, tokens), :] = (k_short[...].astype(F32) * v_input[...].astype(F32)).astype(BF16)

    pl.semaphore_wait(barrier, n - 1)

    def halo(c):
        cols = pl.ds(c * width, width)
        return pltpu.make_async_remote_copy(
            src_ref=ubuf.at[pl.ds(tokens, tokens), cols],
            dst_ref=ubuf.at[pl.ds(0, tokens), cols],
            send_sem=halo_send.at[c],
            recv_sem=halo_recv.at[c],
            device_id={"ctx": lax.rem(me + 1, n)},
            device_id_type=MESH,
        )

    @pl.when(me < n - 1)
    def _():
        for c in range(chunks):
            halo(c).start()

    @pl.when(me == 0)
    def _():
        ubuf[pl.ds(0, tokens), :] = jnp.zeros((tokens, ch), BF16)

    rate = rates[...]
    scaled = weights[...] * jnp.sqrt(2.0 * rate)
    reverse = lax.rem(tokens - iota((1, tokens), 1), tokens).astype(F32)
    total = jnp.zeros((groups, tokens), F32)
    for r in range(order):
        total = total + scaled[:, r : r + 1] * jnp.exp(-rate[:, r : r + 1] * reverse)
    long_row[...] = total
    flip = (lax.rem(iota((tokens, tokens), 0) + iota((tokens, tokens), 1), tokens) == 0).astype(BF16)
    taps_t = jnp.transpose(taps[...].astype(F32)).astype(BF16)
    short_row[...] = jnp.dot(taps_t, flip, preferred_element_type=F32)

    spread = (lax.rem(iota((order, LANES), 1), order) == iota((order, LANES), 0)).astype(F32)
    own = lax.rem(iota((groups, LANES), 0), per) == iota((groups, LANES), 1) // order

    def row_modes(x):
        wide = jnp.dot(x, spread, precision=lax.Precision.HIGHEST, preferred_element_type=F32)
        return jnp.where(own, wide, 0.0)

    rate_wide = row_modes(rate)
    modes[0] = jnp.sum(rate_wide.reshape(blocks, per, LANES), axis=1)
    modes[1] = jnp.sum(row_modes(scaled).reshape(blocks, per, LANES), axis=1)
    rate_tall = jnp.transpose(rate_wide)

    diag = iota((LANES, LANES), 0) // order == iota((LANES, LANES), 1) // share
    lower = iota((tokens, tokens), 0) >= iota((tokens, tokens), 1)

    def compact(x):
        return jnp.sum(jnp.where(diag, x, 0.0).reshape(per, order, LANES), axis=0)

    for b in range(blocks):
        in_block = iota((LANES, groups), 1) // per == b
        column = jnp.sum(jnp.where(in_block, rate_tall, 0.0), axis=1, keepdims=True)
        lam_rc[:, pl.ds(b * LANES, LANES)] = compact(jnp.broadcast_to(column, (LANES, LANES)))
        ahead = (tokens - iota((LANES, tokens), 1)).astype(F32)
        hi, lo = split(jnp.exp(-column * ahead))
        in_tab[b, :, pl.ds(0, tokens)] = hi
        in_tab[b, :, pl.ds(tokens, tokens)] = lo
        rows = iota((tokens, LANES), 0).astype(F32)
        hi, lo = split(modes[1, b : b + 1, :] * jnp.exp(-modes[0, b : b + 1, :] * rows))
        out_tab[b, :, pl.ds(0, LANES)] = hi
        out_tab[b, :, pl.ds(LANES, LANES)] = lo
        out_tab[b, :, pl.ds(2 * LANES, LANES)] = hi

    def tables(b, carry):
        at = pl.multiple_of(b * per, per)
        short8 = short_row[pl.ds(at, per), :]
        long8 = long_row[pl.ds(at, per), :]
        for g in range(per):
            turned = pltpu.roll(
                jnp.broadcast_to(short8[g : g + 1, :], (tokens, tokens)), 0, 1, stride=1, stride_axis=0
            )
            short_tab[b, pl.ds(g * tokens, tokens), pl.ds(0, tokens)] = jnp.where(lower, 0.0, turned).astype(BF16)
            short_tab[b, pl.ds(g * tokens, tokens), pl.ds(tokens, tokens)] = jnp.where(lower, turned, 0.0).astype(BF16)
            turned = pltpu.roll(
                jnp.broadcast_to(long8[g : g + 1, :], (tokens, tokens)), 0, 1, stride=1, stride_axis=0
            )
            long_tab[b, :, pl.ds(g * tokens, tokens)] = jnp.where(lower, turned, 0.0).astype(BF16)
        return carry

    lax.fori_loop(0, blocks, tables, 0)

    lane_group = iota((tokens, LANES), 1) // share

    def short_block(b, carry):
        cols = pl.ds(pl.multiple_of(b * LANES, LANES), LANES)
        full = jnp.dot(short_tab[b], ubuf[:, cols], preferred_element_type=F32)
        y = full[:tokens]
        for g in range(1, per):
            y = jnp.where(lane_group == g, full[g * tokens : (g + 1) * tokens], y)
        u = (k_long[:, cols].astype(F32) * q_short[:, cols].astype(F32) * y).astype(BF16)
        ulong[:, cols] = u
        local = jnp.dot(in_tab[b], jnp.concatenate([u, u], 0), preferred_element_type=F32)
        psend[0, :, cols] = compact(local)
        return carry

    def long_block(b, carry):
        cols = pl.ds(pl.multiple_of(b * LANES, LANES), LANES)
        u = ulong[:, cols]
        wide = jnp.concatenate(
            [jnp.where(lane_group == g, u, jnp.zeros_like(u)) for g in range(per)], 0
        )
        ynear[:, cols] = jnp.dot(long_tab[b], wide, preferred_element_type=F32)
        return carry

    def final_block(b, carry):
        cols = pl.ds(pl.multiple_of(b * LANES, LANES), LANES)
        tall = jnp.where(diag, jnp.concatenate([state[:, cols]] * per, 0), 0.0)
        hi, lo = split(tall)
        far = jnp.dot(out_tab[b], jnp.concatenate([hi, hi, lo], 0), preferred_element_type=F32)
        y = (ynear[:, cols] + far).astype(BF16)
        out[:, cols] = (q_long[:, cols].astype(F32) * y.astype(F32)).astype(BF16)
        return carry

    def scan_copy(k, c, away):
        cols = pl.ds(c * width, width)
        return pltpu.make_async_remote_copy(
            src_ref=psend.at[k, :, cols],
            dst_ref=precv.at[k, :, cols],
            send_sem=scan_send.at[k, c, away],
            recv_sem=scan_recv.at[k, c],
            device_id={"ctx": lax.rem(me + 1 + away, n)},
            device_id_type=MESH,
        )

    def sends(k):
        return lax.rem(me, 2 << k) == (1 << k) - 1

    def scan_send_level(k, c):
        @pl.when(sends(k))
        def _():
            for away in range(1 << k):
                scan_copy(k, c, away).start()

    def scan_take_level(k, c):
        cols = pl.ds(c * width, width)

        @pl.when(lax.rem(me, 2 << k) >= (1 << k))
        def _():
            scan_copy(k, c, 0).wait_recv()
            distance = lax.rem(me, 1 << k) * tokens
            decay = jnp.exp(-lam_rc[:, cols] * distance.astype(F32))
            state[:, cols] = state[:, cols] + decay * precv[k, :, cols]

        if k + 1 < levels:
            decay = jnp.exp(-lam_rc[:, cols] * float(tokens))
            psend[k + 1, :, cols] = psend[0, :, cols] + decay * state[:, cols]

    state[...] = jnp.zeros_like(state)
    for stage in range(chunks + levels):
        if stage < chunks:
            c = stage

            @pl.when(me > 0)
            def _():
                halo(c).wait_recv()

            lax.fori_loop(c * per_chunk, (c + 1) * per_chunk, short_block, 0)
            scan_send_level(0, c)
        for k in range(levels):
            c = stage - 1 - k
            if 0 <= c < chunks:
                scan_take_level(k, c)
                if k + 1 < levels:
                    scan_send_level(k + 1, c)
        c = stage - levels
        if 0 <= stage - 1 < chunks:
            c = stage - 1
            lax.fori_loop(c * per_chunk, (c + 1) * per_chunk, long_block, 0)
    lax.fori_loop(0, blocks, final_block, 0)

    @pl.when(me < n - 1)
    def _():
        for c in range(chunks):
            halo(c).wait_send()

    for k in range(levels):

        @pl.when(sends(k))
        def _():
            for c in range(chunks):
                for away in range(1 << k):
                    scan_copy(k, c, away).wait_send()


def on_device(n, *args):
    q_short, taps, rates = args[0], args[5], args[6]
    tokens, ch = q_short.shape
    groups, order = rates.shape
    blocks = ch // LANES
    per = LANES * groups // ch
    chunks = max(c for c in (1, 2, 4) if blocks % c == 0)
    levels = n.bit_length() - 1
    dma = pltpu.SemaphoreType.DMA
    return pl.pallas_call(
        functools.partial(kernel, n, chunks),
        out_shape=jax.ShapeDtypeStruct((tokens, ch), BF16),
        in_specs=[pl.BlockSpec(memory_space=pltpu.VMEM)] * 8,
        out_specs=pl.BlockSpec(memory_space=pltpu.VMEM),
        scratch_shapes=[
            pltpu.VMEM((2 * tokens, ch), BF16),
            pltpu.VMEM((tokens, ch), BF16),
            pltpu.VMEM((tokens, ch), F32),
            pltpu.VMEM((blocks, per * tokens, 2 * tokens), BF16),
            pltpu.VMEM((blocks, tokens, per * tokens), BF16),
            pltpu.VMEM((blocks, LANES, 2 * tokens), BF16),
            pltpu.VMEM((blocks, tokens, 3 * LANES), BF16),
            pltpu.VMEM((order, ch), F32),
            pltpu.VMEM((groups, tokens), F32),
            pltpu.VMEM((groups, tokens), F32),
            pltpu.VMEM((2, blocks, LANES), F32),
            pltpu.VMEM((order, ch), F32),
            pltpu.VMEM((levels, order, ch), F32),
            pltpu.VMEM((levels, order, ch), F32),
            dma((chunks,)),
            dma((chunks,)),
            dma((levels, chunks, max(1, n // 2))),
            dma((levels, chunks)),
        ],
        compiler_params=pltpu.CompilerParams(
            collective_id=0, has_side_effects=True, vmem_limit_bytes=60 * 2**20
        ),
    )(*args)


def solution(mesh):
    in_specs = (P("ctx", "ch"),) * 5 + (P(None, "ch"), P("ch", None), P("ch", None))
    return jax.shard_map(
        functools.partial(on_device, mesh.shape["ctx"]),
        mesh=mesh,
        in_specs=in_specs,
        out_specs=P("ctx", "ch"),
        check_vma=False,
    )
```

profile of v0, /device:TPU:29, one launch (start us, length us, event | category | flops | bytes accessed | tf_op | source)
XLA Modules:
  0.0 33.3 jit_solution(2942214723571181203)
XLA Ops:
  0.0 0.0 copy-start
  0.0 1.4 %copy.9.rates = f32[128,16]{1,0:T(8,128)} copy(f32[128,16]{0,1:T(8,128)} %param.14) | data formatting | bytes 16384 | tf_op args[6]
  1.4 0.0 copy-done
  1.4 0.7 %copy.10.weights = f32[128,16]{1,0:T(8,128)} copy(f32[128,16]{0,1:T(8,128)S(1)} %copy-done) | data formatting | bytes 16384 | tf_op args[7]
  2.2 29.2 %shard_map.82 = bf16[128,2048]{1,0:T(8,128)(2,1)} custom-call(bf16[128,2048]{1,0:T(8,128)(2,1)} %q_short.1, bf16[128,2048]{1,0:T(8,128)(2,1)} %k_short.1, bf16[128,2048]{1,0:T(8,128)(2,1)} %v_input.1, bf16[128,2048]{1,0:T(8,128)(2,1)} %q_long.1, bf16[128,2048]{1,0:T(8,128)(2,1)} %k_long.1, bf16[128,128]{1,0:T(8,128)(2,1)} %taps.1, f32[128,16]{1,0:T(8,128)} %copy.9.rates, ...), custom_call_target="tpu_custom_call" | custom-call | tf_op jit(solution)/shard_map/pallas_call | solution.py:243
  31.4 1.9 %copy.12 = bf16[128,2048]{1,0:T(8,128)(2,1)} copy(bf16[128,2048]{1,0:T(8,128)(2,1)} %shard_map.82) | data formatting | bytes 1048576
Async XLA Ops:
  0.0 1.4 %copy-start = (f32[128,16]{0,1:T(8,128)S(1)}, f32[128,16]{0,1:T(8,128)}, u32[]{:S(2)}) copy-start(f32[128,16]{0,1:T(8,128)} %param.15) | copy-start | bytes 24580
where the time goes:
time: 33.5 us; the launch traced here: 33.3 us
  Pallas kernels  29.2 us (87%)
  local copies, waits for them, and re-layouts  4.06 us (12%)
    pallas_call x1, Pallas kernels, on_device(): pl.pallas_call(functools.partial(kernel, n, chunks), out_shape=jax.ShapeD...  29.2 us
    unnamed x5, local copies, waits for them, and re-layouts  4.06 us

commit v1 on v0

--- a/solution.py
+++ b/solution.py
@@ -23,13 +23,15 @@
 
 
 def kernel(
-    n, chunks, q_short, k_short, v_input, q_long, k_long, taps, rates, weights, out,
+    n, chunks, q_short_in, k_short, v_input, q_long_in, k_long_in, taps, rates, weights, out,
+    q_short, q_long, k_long, fetch_sem,
     ubuf, ulong, ynear, short_tab, long_tab, in_tab, out_tab, lam_rc, short_row, long_row, modes,
     state, psend, precv, halo_send, halo_recv, scan_send, scan_recv,
 ):
     me = lax.axis_index("ctx")
-    tokens, ch = q_short.shape
-    groups, order = rates.shape
+    tokens, ch = k_short.shape
+    half = tokens // 2
+    order, groups = rates.shape
     share = ch // groups
     per = LANES // share
     blocks = ch // LANES
@@ -42,6 +44,15 @@
         pl.semaphore_signal(
             barrier, inc=1, device_id={"ctx": lax.rem(me + step, n)}, device_id_type=MESH
         )
+
+    fetches = [
+        pltpu.make_async_copy(source, target, fetch_sem.at[i])
+        for i, (source, target) in enumerate(
+            ((q_short_in, q_short), (k_long_in, k_long), (q_long_in, q_long))
+        )
+    ]
+    for fetch in fetches:
+        fetch.start()
 
     ubuf[pl.ds(tokens, tokens), :] = (k_short[...].astype(F32) * v_input[...].astype(F32)).astype(BF16)
 
@@ -67,8 +78,11 @@
     def _():
         ubuf[pl.ds(0, tokens), :] = jnp.zeros((tokens, ch), BF16)
 
-    rate = rates[...]
-    scaled = weights[...] * jnp.sqrt(2.0 * rate)
+    ubuf[pl.ds(2 * tokens, half), :] = jnp.zeros((half, ch), BF16)
+    ulong[pl.ds(0, half), :] = jnp.zeros((half, ch), BF16)
+
+    rate = jnp.transpose(rates[...])
+    scaled = jnp.transpose(weights[...]) * jnp.sqrt(2.0 * rate)
     reverse = lax.rem(tokens - iota((1, tokens), 1), tokens).astype(F32)
     total = jnp.zeros((groups, tokens), F32)
     for r in range(order):
@@ -91,7 +105,9 @@
     rate_tall = jnp.transpose(rate_wide)
 
     diag = iota((LANES, LANES), 0) // order == iota((LANES, LANES), 1) // share
-    lower = iota((tokens, tokens), 0) >= iota((tokens, tokens), 1)
+    rows_half = iota((half, tokens), 0)
+    lower = rows_half >= iota((half, tokens), 1)
+    causal = rows_half + half >= iota((half, tokens), 1)
 
     def compact(x):
         return jnp.sum(jnp.where(diag, x, 0.0).reshape(per, order, LANES), axis=0)
@@ -116,39 +132,47 @@
         long8 = long_row[pl.ds(at, per), :]
         for g in range(per):
             turned = pltpu.roll(
-                jnp.broadcast_to(short8[g : g + 1, :], (tokens, tokens)), 0, 1, stride=1, stride_axis=0
+                jnp.broadcast_to(short8[g : g + 1, :], (half, tokens)), 0, 1, stride=1, stride_axis=0
             )
-            short_tab[b, pl.ds(g * tokens, tokens), pl.ds(0, tokens)] = jnp.where(lower, 0.0, turned).astype(BF16)
-            short_tab[b, pl.ds(g * tokens, tokens), pl.ds(tokens, tokens)] = jnp.where(lower, turned, 0.0).astype(BF16)
+            short_tab[b, pl.ds(g * half, half), pl.ds(0, tokens)] = jnp.where(lower, 0.0, turned).astype(BF16)
+            short_tab[b, pl.ds(g * half, half), pl.ds(tokens, tokens)] = jnp.where(lower, turned, 0.0).astype(BF16)
             turned = pltpu.roll(
-                jnp.broadcast_to(long8[g : g + 1, :], (tokens, tokens)), 0, 1, stride=1, stride_axis=0
+                jnp.broadcast_to(long8[g : g + 1, :], (half, tokens)), half, 1, stride=1, stride_axis=0
             )
-            long_tab[b, :, pl.ds(g * tokens, tokens)] = jnp.where(lower, turned, 0.0).astype(BF16)
+            long_tab[b, :, pl.ds(g * tokens, tokens)] = jnp.where(causal, turned, 0.0).astype(BF16)
         return carry
 
-    lax.fori_loop(0, blocks, tables, 0)
-
-    lane_group = iota((tokens, LANES), 1) // share
+    lax.fori_loop(0, blocks, tables, 0, unroll=2)
+    fetches[0].wait()
+    fetches[1].wait()
+
+    lane_group = lax.rem(iota((half, 2 * LANES), 1), LANES) // share
+    lane_group_tall = lax.rem(iota((tokens, 2 * LANES), 1), LANES) // share
+
+    def windows(x):
+        return jnp.concatenate([x[:, :LANES], x[:, LANES:]], 0)
 
     def short_block(b, carry):
         cols = pl.ds(pl.multiple_of(b * LANES, LANES), LANES)
-        full = jnp.dot(short_tab[b], ubuf[:, cols], preferred_element_type=F32)
-        y = full[:tokens]
+        pair = jnp.concatenate([ubuf[pl.ds(0, 2 * tokens), cols], ubuf[pl.ds(half, 2 * tokens), cols]], 1)
+        full = jnp.dot(short_tab[b], pair, preferred_element_type=F32)
+        y = full[:half]
         for g in range(1, per):
-            y = jnp.where(lane_group == g, full[g * tokens : (g + 1) * tokens], y)
+            y = jnp.where(lane_group == g, full[g * half : (g + 1) * half], y)
+        y = windows(y)
         u = (k_long[:, cols].astype(F32) * q_short[:, cols].astype(F32) * y).astype(BF16)
-        ulong[:, cols] = u
+        ulong[pl.ds(half, tokens), cols] = u
         local = jnp.dot(in_tab[b], jnp.concatenate([u, u], 0), preferred_element_type=F32)
         psend[0, :, cols] = compact(local)
         return carry
 
     def long_block(b, carry):
         cols = pl.ds(pl.multiple_of(b * LANES, LANES), LANES)
-        u = ulong[:, cols]
+        u = jnp.concatenate([ulong[pl.ds(0, tokens), cols], ulong[pl.ds(half, tokens), cols]], 1)
         wide = jnp.concatenate(
-            [jnp.where(lane_group == g, u, jnp.zeros_like(u)) for g in range(per)], 0
-        )
-        ynear[:, cols] = jnp.dot(long_tab[b], wide, preferred_element_type=F32)
+            [jnp.where(lane_group_tall == g, u, jnp.zeros_like(u)) for g in range(per)], 0
+        )
+        ynear[:, cols] = windows(jnp.dot(long_tab[b], wide, preferred_element_type=F32))
         return carry
 
     def final_block(b, carry):
@@ -203,7 +227,7 @@
             def _():
                 halo(c).wait_recv()
 
-            lax.fori_loop(c * per_chunk, (c + 1) * per_chunk, short_block, 0)
+            lax.fori_loop(c * per_chunk, (c + 1) * per_chunk, short_block, 0, unroll=True)
             scan_send_level(0, c)
         for k in range(levels):
             c = stage - 1 - k
@@ -214,8 +238,9 @@
         c = stage - levels
         if 0 <= stage - 1 < chunks:
             c = stage - 1
-            lax.fori_loop(c * per_chunk, (c + 1) * per_chunk, long_block, 0)
-    lax.fori_loop(0, blocks, final_block, 0)
+            lax.fori_loop(c * per_chunk, (c + 1) * per_chunk, long_block, 0, unroll=True)
+    fetches[2].wait()
+    lax.fori_loop(0, blocks, final_block, 0, unroll=4)
 
     @pl.when(me < n - 1)
     def _():
@@ -232,9 +257,10 @@
 
 
 def on_device(n, *args):
+    args = args[:6] + (args[6].T, args[7].T)
     q_short, taps, rates = args[0], args[5], args[6]
     tokens, ch = q_short.shape
-    groups, order = rates.shape
+    order, groups = rates.shape
     blocks = ch // LANES
     per = LANES * groups // ch
     chunks = max(c for c in (1, 2, 4) if blocks % c == 0)
@@ -243,14 +269,18 @@
     return pl.pallas_call(
         functools.partial(kernel, n, chunks),
         out_shape=jax.ShapeDtypeStruct((tokens, ch), BF16),
-        in_specs=[pl.BlockSpec(memory_space=pltpu.VMEM)] * 8,
+        in_specs=[pl.BlockSpec(memory_space=pl.ANY if i in (0, 3, 4) else pltpu.VMEM) for i in range(8)],
         out_specs=pl.BlockSpec(memory_space=pltpu.VMEM),
         scratch_shapes=[
-            pltpu.VMEM((2 * tokens, ch), BF16),
             pltpu.VMEM((tokens, ch), BF16),
+            pltpu.VMEM((tokens, ch), BF16),
+            pltpu.VMEM((tokens, ch), BF16),
+            dma((3,)),
+            pltpu.VMEM((2 * tokens + tokens // 2, ch), BF16),
+            pltpu.VMEM((tokens + tokens // 2, ch), BF16),
             pltpu.VMEM((tokens, ch), F32),
-            pltpu.VMEM((blocks, per * tokens, 2 * tokens), BF16),
-            pltpu.VMEM((blocks, tokens, per * tokens), BF16),
+            pltpu.VMEM((blocks, per * tokens // 2, 2 * tokens), BF16),
+            pltpu.VMEM((blocks, tokens // 2, per * tokens), BF16),
             pltpu.VMEM((blocks, LANES, 2 * tokens), BF16),
             pltpu.VMEM((blocks, tokens, 3 * LANES), BF16),
             pltpu.VMEM((order, ch), F32),

time: 33.5 us -> 23.8 us (0.71)
  Pallas kernels: 29.2 us -> 21.7 us
  local copies, waits for them, and re-layouts: 4.06 us -> 1.88 us
    pallas_call x1, Pallas kernels: 29.2 us -> 21.7 us  [on_device(): pl.pallas_call(functools.partial(kernel, n, chunks), out_shape=jax.ShapeD...]
    unnamed x5 -> x1, local copies, waits for them, and re-layouts: 4.06 us -> 1.88 us
where the time goes in v1:
time: 23.8 us; the launch traced here: 23.6 us
  Pallas kernels  21.7 us (91%)
  local copies, waits for them, and re-layouts  1.88 us (8%)
    pallas_call x1, Pallas kernels, on_device(): pl.pallas_call(functools.partial(kernel, n, chunks), out_shape=jax.ShapeD...  21.7 us
    unnamed x1, local copies, waits for them, and re-layouts  1.88 us

profile of v1, /device:TPU:29, one launch (start us, length us, event | category | flops | bytes accessed | tf_op | source)
XLA Modules:
  0.0 23.6 jit_solution(2863605035782895693)
XLA Ops:
  0.0 21.7 %shard_map.82 = bf16[128,2048]{1,0:T(8,128)(2,1)} custom-call(bf16[128,2048]{1,0:T(8,128)(2,1)} %q_short_in.1, bf16[128,2048]{1,0:T(8,128)(2,1)} %k_short.1, bf16[128,2048]{1,0:T(8,128)(2,1)} %v_input.1, bf16[128,2048]{1,0:T(8,128)(2,1)} %q_long_in.1, bf16[128,2048]{1,0:T(8,128)(2,1)} %k_long_in.1, bf16[128,128]{1,0:T(8,128)(2,1)} %taps.1, ...), custom_call_target="tpu_custom_call" | custom-call | tf_op jit(solution)/shard_map/pallas_call | solution.py:269
  21.7 1.9 %copy.10 = bf16[128,2048]{1,0:T(8,128)(2,1)} copy(bf16[128,2048]{1,0:T(8,128)(2,1)} %shard_map.82) | data formatting | bytes 1048576

commit v2 on v1

--- a/solution.py
+++ b/solution.py
@@ -218,29 +218,43 @@
             decay = jnp.exp(-lam_rc[:, cols] * float(tokens))
             psend[k + 1, :, cols] = psend[0, :, cols] + decay * state[:, cols]
 
-    state[...] = jnp.zeros_like(state)
-    for stage in range(chunks + levels):
-        if stage < chunks:
-            c = stage
-
-            @pl.when(me > 0)
-            def _():
-                halo(c).wait_recv()
-
-            lax.fori_loop(c * per_chunk, (c + 1) * per_chunk, short_block, 0, unroll=True)
-            scan_send_level(0, c)
+    def over(c, body):
+        lax.fori_loop(c * per_chunk, (c + 1) * per_chunk, body, 0, unroll=True)
+
+    def takes(stage):
         for k in range(levels):
             c = stage - 1 - k
             if 0 <= c < chunks:
                 scan_take_level(k, c)
                 if k + 1 < levels:
                     scan_send_level(k + 1, c)
-        c = stage - levels
-        if 0 <= stage - 1 < chunks:
-            c = stage - 1
-            lax.fori_loop(c * per_chunk, (c + 1) * per_chunk, long_block, 0, unroll=True)
+
+    state[...] = jnp.zeros_like(state)
+    for c in range(chunks):
+
+        @pl.when(me > 0)
+        def _():
+            halo(c).wait_recv()
+
+        over(c, short_block)
+        scan_send_level(0, c)
+        takes(c)
     fetches[2].wait()
-    lax.fori_loop(0, blocks, final_block, 0, unroll=4)
+    nears, ends = 0, 0
+    for step in range(levels):
+        stage = chunks + step
+        goal = -(-chunks * (step + 1) // levels)
+        while nears < goal:
+            over(nears, long_block)
+            nears += 1
+        while ends < min(nears, stage - levels):
+            over(ends, final_block)
+            ends += 1
+        takes(stage)
+    for c in range(nears, chunks):
+        over(c, long_block)
+    for c in range(ends, chunks):
+        over(c, final_block)
 
     @pl.when(me < n - 1)
     def _():

time: 23.8 us -> 22.3 us (0.937)
  Pallas kernels: 21.7 us -> 20.3 us
    pallas_call x1, Pallas kernels: 21.7 us -> 20.3 us  [on_device(): pl.pallas_call(functools.partial(kernel, n, chunks), out_shape=jax.ShapeD...]
where the time goes in v2:
time: 22.3 us; the launch traced here: 22.2 us
  Pallas kernels  20.3 us (91%)
  local copies, waits for them, and re-layouts  1.88 us (8%)
    pallas_call x1, Pallas kernels, on_device(): pl.pallas_call(functools.partial(kernel, n, chunks), out_shape=jax.ShapeD...  20.3 us
    unnamed x1, local copies, waits for them, and re-layouts  1.88 us

profile of v2, /device:TPU:29, one launch (start us, length us, event | category | flops | bytes accessed | tf_op | source)
XLA Modules:
  0.0 22.2 jit_solution(12002968582810994647)
XLA Ops:
  0.0 20.3 %shard_map.82 = bf16[128,2048]{1,0:T(8,128)(2,1)} custom-call(bf16[128,2048]{1,0:T(8,128)(2,1)} %q_short_in.1, bf16[128,2048]{1,0:T(8,128)(2,1)} %k_short.1, bf16[128,2048]{1,0:T(8,128)(2,1)} %v_input.1, bf16[128,2048]{1,0:T(8,128)(2,1)} %q_long_in.1, bf16[128,2048]{1,0:T(8,128)(2,1)} %k_long_in.1, bf16[128,128]{1,0:T(8,128)(2,1)} %taps.1, ...), custom_call_target="tpu_custom_call" | custom-call | tf_op jit(solution)/shard_map/pallas_call | solution.py:283
  20.3 1.9 %copy.10 = bf16[128,2048]{1,0:T(8,128)(2,1)} copy(bf16[128,2048]{1,0:T(8,128)(2,1)} %shard_map.82) | data formatting | bytes 1048576

commit v3 on v2

--- a/solution.py
+++ b/solution.py
@@ -23,13 +23,13 @@
 
 
 def kernel(
-    n, chunks, q_short_in, k_short, v_input, q_long_in, k_long_in, taps, rates, weights, out,
-    q_short, q_long, k_long, fetch_sem,
+    n, chunks, q_short_in, k_short_in, v_input_in, q_long_in, k_long_in, taps, rates, weights, out,
+    q_short, q_long, k_long, k_short, v_input, fetch_sem,
     ubuf, ulong, ynear, short_tab, long_tab, in_tab, out_tab, lam_rc, short_row, long_row, modes,
     state, psend, precv, halo_send, halo_recv, scan_send, scan_recv,
 ):
     me = lax.axis_index("ctx")
-    tokens, ch = k_short.shape
+    tokens, ch = k_short_in.shape
     half = tokens // 2
     order, groups = rates.shape
     share = ch // groups
@@ -48,11 +48,19 @@
     fetches = [
         pltpu.make_async_copy(source, target, fetch_sem.at[i])
         for i, (source, target) in enumerate(
-            ((q_short_in, q_short), (k_long_in, k_long), (q_long_in, q_long))
+            (
+                (q_short_in, q_short),
+                (k_long_in, k_long),
+                (q_long_in, q_long),
+                (k_short_in, k_short),
+                (v_input_in, v_input),
+            )
         )
     ]
-    for fetch in fetches:
-        fetch.start()
+    for i in (3, 4, 0, 1, 2):
+        fetches[i].start()
+    fetches[3].wait()
+    fetches[4].wait()
 
     ubuf[pl.ds(tokens, tokens), :] = (k_short[...].astype(F32) * v_input[...].astype(F32)).astype(BF16)
 
@@ -283,13 +291,15 @@
     return pl.pallas_call(
         functools.partial(kernel, n, chunks),
         out_shape=jax.ShapeDtypeStruct((tokens, ch), BF16),
-        in_specs=[pl.BlockSpec(memory_space=pl.ANY if i in (0, 3, 4) else pltpu.VMEM) for i in range(8)],
+        in_specs=[pl.BlockSpec(memory_space=pl.ANY if i < 5 else pltpu.VMEM) for i in range(8)],
         out_specs=pl.BlockSpec(memory_space=pltpu.VMEM),
         scratch_shapes=[
             pltpu.VMEM((tokens, ch), BF16),
             pltpu.VMEM((tokens, ch), BF16),
             pltpu.VMEM((tokens, ch), BF16),
-            dma((3,)),
+            pltpu.VMEM((tokens, ch), BF16),
+            pltpu.VMEM((tokens, ch), BF16),
+            dma((5,)),
             pltpu.VMEM((2 * tokens + tokens // 2, ch), BF16),
             pltpu.VMEM((tokens + tokens // 2, ch), BF16),
             pltpu.VMEM((tokens, ch), F32),

time: 22.3 us -> 22 us (0.987)
  Pallas kernels: 20.3 us -> 19.9 us
    pallas_call x1, Pallas kernels: 20.3 us -> 19.9 us  [on_device(): pl.pallas_call(functools.partial(kernel, n, chunks), out_shape=jax.ShapeD...]
where the time goes in v3:
time: 22 us; the launch traced here: 21.7 us
  Pallas kernels  19.9 us (90%)
  local copies, waits for them, and re-layouts  1.88 us (9%)
    pallas_call x1, Pallas kernels, on_device(): pl.pallas_call(functools.partial(kernel, n, chunks), out_shape=jax.ShapeD...  19.9 us
    unnamed x1, local copies, waits for them, and re-layouts  1.88 us

profile of v3, /device:TPU:29, one launch (start us, length us, event | category | flops | bytes accessed | tf_op | source)
XLA Modules:
  0.0 21.7 jit_solution(890942540177403846)
XLA Ops:
  0.0 19.9 %shard_map.82 = bf16[128,2048]{1,0:T(8,128)(2,1)} custom-call(bf16[128,2048]{1,0:T(8,128)(2,1)} %q_short_in.1, bf16[128,2048]{1,0:T(8,128)(2,1)} %k_short_in.1, bf16[128,2048]{1,0:T(8,128)(2,1)} %v_input_in.1, bf16[128,2048]{1,0:T(8,128)(2,1)} %q_long_in.1, bf16[128,2048]{1,0:T(8,128)(2,1)} %k_long_in.1, bf16[128,128]{1,0:T(8,128)(2,1)} %taps.1, ...), custom_call_target="tpu_custom_call" | custom-call | tf_op jit(solution)/shard_map/pallas_call | solution.py:291
  19.9 1.9 %copy.10 = bf16[128,2048]{1,0:T(8,128)(2,1)} copy(bf16[128,2048]{1,0:T(8,128)(2,1)} %shard_map.82) | data formatting | bytes 1048576

commit v4 on v3

--- a/solution.py
+++ b/solution.py
@@ -57,10 +57,12 @@
             )
         )
     ]
-    for i in (3, 4, 0, 1, 2):
+    for i in (3, 4):
         fetches[i].start()
     fetches[3].wait()
     fetches[4].wait()
+    for i in (0, 1, 2):
+        fetches[i].start()
 
     ubuf[pl.ds(tokens, tokens), :] = (k_short[...].astype(F32) * v_input[...].astype(F32)).astype(BF16)
 

time: 22 us -> 22 us (level)
  no operation moved by 1% of the time
where the time goes in v4:
time: 22 us; the launch traced here: 21.7 us
  Pallas kernels  19.9 us (90%)
  local copies, waits for them, and re-layouts  1.88 us (9%)
    pallas_call x1, Pallas kernels, on_device(): pl.pallas_call(functools.partial(kernel, n, chunks), out_shape=jax.ShapeD...  19.9 us
    unnamed x1, local copies, waits for them, and re-layouts  1.88 us

profile of v4, /device:TPU:29, one launch (start us, length us, event | category | flops | bytes accessed | tf_op | source)
XLA Modules:
  0.0 21.7 jit_solution(4721110997641152640)
XLA Ops:
  0.0 19.9 %shard_map.82 = bf16[128,2048]{1,0:T(8,128)(2,1)} custom-call(bf16[128,2048]{1,0:T(8,128)(2,1)} %q_short_in.1, bf16[128,2048]{1,0:T(8,128)(2,1)} %k_short_in.1, bf16[128,2048]{1,0:T(8,128)(2,1)} %v_input_in.1, bf16[128,2048]{1,0:T(8,128)(2,1)} %q_long_in.1, bf16[128,2048]{1,0:T(8,128)(2,1)} %k_long_in.1, bf16[128,128]{1,0:T(8,128)(2,1)} %taps.1, ...), custom_call_target="tpu_custom_call" | custom-call | tf_op jit(solution)/shard_map/pallas_call | solution.py:293
  19.9 1.9 %copy.10 = bf16[128,2048]{1,0:T(8,128)(2,1)} copy(bf16[128,2048]{1,0:T(8,128)(2,1)} %shard_map.82) | data formatting | bytes 1048576
